TPU v7x, 128 devices: a whole 4x4x4 slice. The times are simulated.
128 devices in a mesh: group: 16 (over x, z_hi, core), inner: 8 (over z_lo, y).
Axes of the slice: x: 4, y: 4, z: 4 (z_hi: 2, z_lo: 2; z = z_hi * 2 + z_lo), core: 2. Of those that a mesh axis runs over, the one named last changes fastest.
Arguments:
- tokens: bfloat16 [16, 512, 2304], P('group', 'inner'), may hold values from -6 to 6
- lengths: int32 [16], P('group'), may hold values from 1 to 512, 5120 in all
- tenant_cut: int32 [16], P('group'), may hold values from 64 to 255
- expert_ids: int32 [16, 512, 2], P('group', 'inner'), may hold values from 0 to 7, all different within a row; in each aligned block of 64 rows (0 to 63, 64 to 127, ..., all dimensions but the last counted through in order) at most 20 rows name the same one
- trainer_qkv: float32 [2304, 3, 2048], P(('group', 'inner')), may hold values from -0.26 to 0.26
- trainer_gate_up: float32 [8, 2304, 2, 5760], P(None, ('group', 'inner')), may hold values from -0.125 to 0.125
- out_weight: bfloat16 [2048, 2304], P('inner'), may hold values from -0.75 to 0.75
- down_weight: bfloat16 [8, 5760, 2304], P('inner', 'group'), may hold values from -0.078125 to 0.078125
- attn_gain: float32 [2304], replicated, may hold values from 0.1 to 1.9
- moe_gain: float32 [2304], replicated, may hold values from 0.1 to 1.9
- router: bfloat16 [2304, 8], replicated, may hold values from -0.375 to 0.375
Outputs:
- server_qkv: bfloat16 [2304, 3, 2048], P(None, None, 'inner')
- server_gate_up: bfloat16 [8, 2304, 2, 5760], P('inner', None, None, 'group')
- layer_out: bfloat16 [16, 512, 2304], P('group', 'inner')
Inputs may be any that keep to these rules, and one draw needn't show every extreme that they name: `expert_ids`: in each aligned block of 64 token slots (the slots of one device) no expert is named more than 20 times, a bound that some block reaches. The two experts of a slot differ. `lengths`: some prompt uses all 512 slots.
All inputs are finite; a program needn't handle non-finite values. No bound on the sum of `lengths` on one device may be relied on, other than what follows from the above.
Results may differ from a plain program's by a relative error of at most 0.015.
Values may be sent and summed in bfloat16 or wider, within the bound.
A program may use at most 128 MiB of HBM per device.

v0:
```python
import math
import jax
import jax.numpy as jnp
from jax import lax
from jax.sharding import PartitionSpec as P

D = 2304
HEAD_DIM = 64
TOPK = 2
NORM_EPS = 1e-05
MASKED = -1e30


def rms_scaled(values, gain_row):
    mean_square = jnp.mean(values * values, axis=-1, keepdims=True)
    return values * lax.rsqrt(mean_square + NORM_EPS) * gain_row


def token_layout(length, cut_point, total):
    places = jnp.arange(total, dtype=jnp.int32)
    beyond = places >= length
    second = places >= cut_point
    starts = jnp.where(beyond, length, jnp.where(second, cut_point, 0))
    tenants = jnp.where(beyond, 2, jnp.where(second, 1, 0))
    return (places - starts, tenants, places)


def rotate_heads(values, positions):
    half_dim = values.shape[-1] // 2
    freqs = jnp.exp(-math.log(10000.0) * jnp.arange(half_dim, dtype=jnp.float32) / half_dim)
    angles = positions.astype(jnp.float32)[:, None] * freqs[None, :]
    cosine = jnp.cos(angles)[:, None, :]
    sine = jnp.sin(angles)[:, None, :]
    first_half = values[..., :half_dim]
    second_half = values[..., half_dim:]
    return jnp.concatenate(
        [first_half * cosine - second_half * sine, second_half * cosine + first_half * sine],
        axis=-1,
    )


def body(
    tokens,
    lengths,
    tenant_cut,
    expert_ids,
    trainer_qkv,
    trainer_gate_up,
    out_weight,
    down_weight,
    attn_gain,
    moe_gain,
    router,
):
    group_size = lax.axis_size("group")
    inner_size = lax.axis_size("inner")
    row_share = trainer_qkv.shape[0]
    head_block = trainer_qkv.shape[2] // inner_size
    cast_qkv = trainer_qkv.astype(jnp.bfloat16).reshape(row_share, 3, inner_size, head_block)
    head_parts = lax.all_to_all(cast_qkv, "inner", split_axis=2, concat_axis=0, tiled=True)
    head_parts = head_parts.reshape(inner_size * row_share, 3, head_block)
    server_qkv = lax.all_gather(head_parts, "group", axis=0, tiled=True)
    expert_count = trainer_gate_up.shape[0]
    local_experts = expert_count // inner_size
    hidden_share = trainer_gate_up.shape[3] // group_size
    cast_gate_up = trainer_gate_up.astype(jnp.bfloat16).reshape(
        inner_size, local_experts, row_share, 2, group_size, hidden_share
    )
    ordered = jnp.transpose(cast_gate_up, (4, 0, 1, 2, 3, 5))
    joined = ordered.reshape(group_size * inner_size, local_experts, 1, row_share, 2, hidden_share)
    moved = lax.all_to_all(joined, ("group", "inner"), split_axis=0, concat_axis=2, tiled=True)
    server_gate_up = moved.reshape(local_experts, D, 2, hidden_share)
    tok_rows = tokens.shape[1]
    own_inputs = tokens[0].astype(jnp.float32)
    normed = rms_scaled(own_inputs, attn_gain).astype(jnp.bfloat16)
    length = lengths[0]
    cut_point = tenant_cut[0]
    heads_here = head_block // HEAD_DIM
    flat_qkv = server_qkv.reshape(D, 3 * head_block)
    piece_rows = lax.all_gather(normed, "inner", axis=0, tiled=True)
    row_count = piece_rows.shape[0]
    raw = jnp.dot(piece_rows, flat_qkv, preferred_element_type=jnp.float32).reshape(
        row_count, 3, heads_here, HEAD_DIM
    )
    positions, unused_tenants, unused_places = token_layout(length, cut_point, row_count)
    queries = rotate_heads(raw[:, 0], positions).astype(jnp.bfloat16)
    keys_rot = rotate_heads(raw[:, 1], positions).astype(jnp.bfloat16)
    values_v = raw[:, 2].astype(jnp.bfloat16)
    packed = jnp.stack([queries, keys_rot, values_v], axis=1).reshape(row_count, 3, head_block)
    seq_len = packed.shape[0]
    packed = packed.reshape(seq_len, 3, heads_here, HEAD_DIM)
    queries = packed[:, 0]
    keys_rot = packed[:, 1]
    values_v = packed[:, 2]
    unused_positions, tenants, places = token_layout(length, cut_point, seq_len)
    block_rows = min(seq_len, 512)
    scores = jnp.einsum(
        "qhd,khd->hqk", queries, keys_rot, preferred_element_type=jnp.float32
    ) / math.sqrt(HEAD_DIM)
    allowed = (tenants[0:block_rows, None] == tenants[None, :]) & (
        places[None, :] <= places[0:block_rows, None]
    )
    scores = jnp.where(allowed[None], scores, MASKED)
    weights = jax.nn.softmax(scores, axis=-1).astype(jnp.bfloat16)
    mixed = jnp.einsum("hqk,khd->qhd", weights, values_v, preferred_element_type=jnp.float32)
    block_outputs = mixed.astype(jnp.bfloat16).reshape(block_rows, head_block)
    projected = lax.psum_scatter(
        jnp.dot(block_outputs, out_weight, preferred_element_type=jnp.float32),
        "inner",
        scatter_dimension=0,
        tiled=True,
    )
    residual = own_inputs + projected
    normed_moe = rms_scaled(residual, moe_gain).astype(jnp.bfloat16)
    logits = jnp.dot(normed_moe, router, preferred_element_type=jnp.float32)
    route_ids = expert_ids[0]
    expert_range = jnp.arange(expert_count, dtype=jnp.int32)
    onehot = route_ids[:, :, None] == expert_range[None, None, :]
    chosen = jnp.sum(jnp.where(onehot, logits[:, None, :], 0.0), axis=-1)
    first_weight = jax.nn.sigmoid(chosen[:, 0] - chosen[:, 1])
    capacity = tok_rows * 5 // 16
    flat_hot = onehot.reshape(tok_rows * TOPK, expert_count).astype(jnp.int32)
    ranks = jnp.cumsum(flat_hot, axis=0) - flat_hot
    slot_ids = jnp.sum((expert_range[None, :] * capacity + ranks) * flat_hot, axis=1)
    slot_range = jnp.arange(expert_count * capacity, dtype=jnp.int32)
    dispatch = (slot_ids[None, :] == slot_range[:, None]).astype(jnp.bfloat16)
    repeated = jnp.broadcast_to(normed_moe[:, None, :], (tok_rows, TOPK, D)).reshape(
        tok_rows * TOPK, D
    )
    send_rows = jnp.dot(dispatch, repeated, preferred_element_type=jnp.float32).astype(jnp.bfloat16)
    send_rows = send_rows.reshape(inner_size, local_experts, capacity, D)
    owned = lax.all_to_all(send_rows, "inner", split_axis=0, concat_axis=0, tiled=True)
    arrived = lax.all_gather(owned, "group", axis=0, tiled=True)
    item_count = arrived.shape[0]
    rows_in = arrived[:, 0].reshape(item_count * capacity, D)
    both = jnp.dot(
        rows_in, server_gate_up[0].reshape(D, 2 * hidden_share), preferred_element_type=jnp.float32
    )
    both = both.reshape(item_count * capacity, 2, hidden_share)
    hidden = (jax.nn.silu(both[:, 0]) * both[:, 1]).astype(jnp.bfloat16)
    down_part = jnp.dot(hidden, down_weight[0], preferred_element_type=jnp.float32)
    results = [down_part.reshape(item_count, capacity, D)]
    terms = jnp.stack(results, axis=1).astype(jnp.bfloat16)
    summed = lax.psum_scatter(terms, "group", scatter_dimension=0, tiled=True).astype(jnp.float32)
    expert_out = lax.all_to_all(
        summed.astype(jnp.bfloat16), "inner", split_axis=0, concat_axis=0, tiled=True
    )
    flat_out = expert_out.reshape(expert_count * capacity, D)
    route_slots = slot_ids.reshape(tok_rows, TOPK)
    pick_first = (route_slots[:, 0:1] == slot_range[None, :]).astype(jnp.bfloat16)
    pick_second = (route_slots[:, 1:2] == slot_range[None, :]).astype(jnp.bfloat16)
    first_out = jnp.dot(pick_first, flat_out, preferred_element_type=jnp.float32)
    second_out = jnp.dot(pick_second, flat_out, preferred_element_type=jnp.float32)
    moe = first_weight[:, None] * first_out + (1.0 - first_weight)[:, None] * second_out
    combined = residual + moe
    own_places = lax.axis_index("inner") * tok_rows + jnp.arange(tok_rows, dtype=jnp.int32)
    layer_out = jnp.where((own_places < length)[:, None], combined, 0.0).astype(jnp.bfloat16)
    return (server_qkv, server_gate_up, layer_out[None])


def solution(mesh):
    placed = (
        P("group", "inner", None),
        P("group"),
        P("group"),
        P("group", "inner", None),
        P(("group", "inner"), None, None),
        P(None, ("group", "inner"), None, None),
        P("inner", None),
        P("inner", "group", None),
        P(),
        P(),
        P(),
    )
    return jax.shard_map(
        body,
        mesh=mesh,
        in_specs=placed,
        out_specs=(
            P(None, None, "inner"),
            P("inner", None, None, "group"),
            P("group", "inner", None),
        ),
        check_vma=False,
    )
```

profile of v0, /device:TPU:1, one launch (start us, length us, event | category | flops | bytes accessed | tf_op | source)
XLA Modules:
  0.0 555.8 jit_solution(7805670884036663510)
XLA Ops:
  8.9 12.7 %all_to_all.34 = bf16[18,3,8,256]{3,0,1,2:T(8,128)(2,1)S(1)} all-to-all(bf16[18,3,8,256]{3,0,1,2:T(8,128)(2,1)S(1)} %copy.52), channel_id=1, replica_groups=mesh['group'=16,'inner'=8] {'inner'}, dimensions={2} | all-to-all | bytes 442368 | tf_op jit(solution)/shard_map/all_to_all | solution.py:60
  26.8 51.4 %all-gather.4.cloned.1.call-done = bf16[2304,3,256]{2,0,1:T(8,128)(2,1)} async-done(((bf16[144,3,256]{2,0,1:T(8,128)(2,1)}), bf16[2304,3,256]{2,0,1:T(8,128)(2,1)}) %all-gather.4.cloned.1.call-update) | async-done | bytes 3538960 | tf_op jit(solution)/shard_map/all_gather | solution.py:62
  78.2 5.7 %copy.55 = bf16[2304,3,256]{0,2,1:T(8,128)(2,1)} copy(bf16[2304,3,256]{2,0,1:T(8,128)(2,1)} %all-gather.4.cloned.1.call-done) | data formatting | bytes 7077888 | tf_op jit(solution)/shard_map/all_gather | solution.py:62
  84.0 31.8 %all-gather.6.cloned.1.call-done = bf16[512,2304]{1,0:T(8,128)(2,1)} async-done(((bf16[64,2304]{1,0:T(8,128)(2,1)}), bf16[512,2304]{1,0:T(8,128)(2,1)}) %all-gather.6.cloned.1.call-update) | async-done | bytes 2359312 | tf_op jit(solution)/shard_map/all_gather | solution.py:80
  115.8 4.8 fusion.8
  121.6 4.8 fusion.36
  133.6 61.1 %reduce-scatter.5.cloned.1.call-done = f32[64,2304]{1,0:T(8,128)} async-done(((f32[512,2304]{1,0:T(8,128)}), f32[64,2304]{1,0:T(8,128)}) %reduce-scatter.5.cloned.1.call-update) | async-done | bytes 589840 | tf_op jit(solution)/shard_map/reduce_scatter | solution.py:107
  200.9 16.1 %all_to_all.35 = bf16[8,1,20,2304]{3,2,1,0:T(8,128)(2,1)S(1)} all-to-all(bf16[8,1,20,2304]{3,2,1,0:T(8,128)(2,1)S(1)} %bitcast.90), channel_id=1, replica_groups=mesh['group'=16,'inner'=8] {'inner'}, dimensions={0} | all-to-all | bytes 1474560 | tf_op jit(solution)/shard_map/all_to_all | solution.py:132
  218.2 6.9 %convert_element_type.69 = bf16[8,18,2,5760]{3,2,1,0:T(2,128)(2,1)} convert(f32[8,18,2,5760]{3,2,1,0:T(2,128)} %param.16) | non-fusion elementwise | flops 1658880 | bytes 9953280 | tf_op jit(solution)/shard_map/convert_element_type | solution.py:66
  225.1 11.5 %reshape.215 = bf16[8,1,18,2,16,360]{5,4,3,2,0,1:T(8,128)(2,1)} reshape(bf16[8,18,2,5760]{3,2,1,0:T(2,128)(2,1)} %convert_element_type.69) | data formatting | bytes 6635520 | tf_op jit(solution)/shard_map/reshape | solution.py:66
  236.6 4.7 copy.54
  241.4 61.6 %all_to_all.36 = bf16[128,1,1,18,2,360]{5,4,3,2,1,0:T(2,128)(2,1)} all-to-all(bf16[128,1,1,18,2,360]{5,4,3,2,1,0:T(2,128)(2,1)S(1)} %bitcast.87), channel_id=1, replica_groups=mesh['group'=16,'inner'=8] {'group','inner'}, dimensions={0} | all-to-all | bytes 6635520 | tf_op jit(solution)/shard_map/all_to_all | solution.py:71
  302.9 8.5 %reshape_squeeze_reshape.3 = bf16[2304,720]{1,0:T(8,128)(2,1)} reshape(bf16[128,1,1,18,2,360]{5,4,3,2,1,0:T(2,128)(2,1)} %all_to_all.36) | data formatting | bytes 6635520 | tf_op jit(solution)/shard_map/reshape;squeeze;reshape | solution.py:137
  311.4 5.6 %copy.61 = bf16[720,2304]{1,0:T(8,128)(2,1)} copy(bf16[720,2304]{0,1:T(8,128)(2,1)} %bitcast.88) | data formatting | bytes 6635520 | tf_op jit(solution)/shard_map/dot_general | solution.py:136
  317.1 24.8 %all-gather.8.cloned.1.call-done = bf16[128,1,20,2304]{3,0,2,1:T(8,128)(2,1)} async-done(((bf16[8,1,20,2304]{3,0,2,1:T(8,128)(2,1)}), bf16[128,1,20,2304]{3,0,2,1:T(8,128)(2,1)}) %all-gather.8.cloned.1.call-update) | async-done | bytes 11796496 | tf_op jit(solution)/shard_map/all_gather | solution.py:133
  341.9 14.9 %copy.60 = bf16[128,1,20,2304]{3,2,0,1:T(8,128)(2,1)} copy(bf16[128,1,20,2304]{3,0,2,1:T(8,128)(2,1)} %all-gather.8.cloned.1.call-done) | data formatting | bytes 23592960 | tf_op jit(solution)/shard_map/all_gather | solution.py:133
  356.7 17.2 %reshape.226 = bf16[2560,2304,1]{1,0,2:T(8,128)(2,1)} reshape(bf16[128,1,20,2304]{3,2,0,1:T(8,128)(2,1)} %copy.60) | data formatting | bytes 23592960 | tf_op jit(solution)/shard_map/reshape;squeeze | solution.py:135
  373.9 12.7 %fusion.44 = f32[2560,2,360]{0,2,1:T(8,128)S(1)} fusion(bf16[2560,2304,1]{1,0,2:T(8,128)(2,1)} %reshape.226, bf16[2,360,2304]{2,1,0:T(8,128)(2,1)} %bitcast.91), kind=kOutput, calls=%fused_computation.81 | convolution fusion | flops 8493465600 | bytes 22487040 | tf_op jit(solution)/shard_map/dot_general | solution.py:136
  392.8 4.0 convert_element_type.82
  396.8 8.3 %fusion.37 = bf16[16,8,20,2304]{3,1,0,2:T(8,128)(2,1)S(1)} fusion(bf16[1,360,2304]{2,1,0:T(8,128)(2,1)S(1)} %copy-done, bf16[128,20,360]{2,1,0:T(8,128)(2,1)} %convert_element_type.82), kind=kOutput, calls=%fused_computation.78 | convolution fusion | flops 4252631040 | bytes 15298560 | tf_op jit(solution)/shard_map/dot_general | solution.py:141
  405.1 5.0 copy.72
  410.5 113.2 %reduce-scatter.7.cloned.1.call-done = bf16[8,46080]{1,0:T(8,128)(2,1)} async-done(((bf16[128,46080]{1,0:T(8,128)(2,1)}), bf16[8,46080]{1,0:T(8,128)(2,1)}) %reduce-scatter.7.cloned.1.call-update) | async-done | bytes 737296
  525.8 4.2 all-to-all-start.3
  530.1 10.4 %copy.65 = bf16[1,2304,2,360]{1,3,2,0:T(8,128)(2,1)} copy(bf16[1,2304,2,360]{3,2,1,0:T(2,128)(2,1)} %bitcast.86) | data formatting | bytes 6635520
  (80 shorter events, 38.4 us)
Async XLA Ops:
  7.2 389.6 %copy-start = (bf16[1,360,2304]{2,1,0:T(8,128)(2,1)S(1)}, bf16[1,360,2304]{2,1,0:T(8,128)(2,1)}, u32[]{:S(2)}) copy-start(bf16[1,360,2304]{2,1,0:T(8,128)(2,1)} %param.18) | copy-start | bytes 4976644
  7.2 15.3 %copy-start.2 = (bf16[1,64,2304]{2,1,0:T(8,128)(2,1)S(1)}, bf16[1,64,2304]{2,1,0:T(8,128)(2,1)}, u32[]{:S(2)}) copy-start(bf16[1,64,2304]{2,1,0:T(8,128)(2,1)} %param.11) | copy-start | bytes 884740
  7.2 15.5 %copy-start.11 = (f32[2304]{0:T(1024)S(1)}, f32[2304]{0:T(1024)}, u32[]{:S(2)}) copy-start(f32[2304]{0:T(1024)} %param.19) | copy-start | bytes 27652
  7.2 71.0 %all-gather.4.cloned.1.call-start = ((), (), s32[]{:S(2)}) async-start(), calls=%async_computation.6 | async-start | bytes 3760128 | tf_op jit(solution)/shard_map/all_gather | solution.py:62
  22.4 93.4 %all-gather.6.cloned.1.call-start = ((), (), s32[]{:S(2)}) async-start(), calls=%async_computation.7 | async-start | bytes 2654208 | tf_op jit(solution)/shard_map/all_gather | solution.py:80
  23.5 171.1 %reduce-scatter.5.cloned.1.call-start = ((), (), s32[]{:S(2)}) async-start(), calls=%async_computation.8 | async-start | bytes 5308416 | tf_op jit(solution)/shard_map/reduce_scatter | solution.py:107
  115.8 4.9 copy-start.7
  115.8 4.9 copy-start.8
  126.5 2.8 copy-start.6
  132.2 0.7 copy-start.12
  132.2 63.7 %copy-start.10 = (f32[2304]{0:T(1024)S(1)}, f32[2304]{0:T(1024)}, u32[]{:S(2)}) copy-start(f32[2304]{0:T(1024)} %param.20) | copy-start | bytes 27652
  132.3 209.6 %all-gather.8.cloned.1.call-start = ((), (), s32[]{:S(2)}) async-start(), calls=%async_computation.9 | async-start | bytes 12533760 | tf_op jit(solution)/shard_map/all_gather | solution.py:133
  197.1 0.7 copy-start.4
  218.0 305.7 %reduce-scatter.7.cloned.1.call-start = ((), (), s32[]{:S(2)}) async-start(), calls=%async_computation.10 | async-start | bytes 12533760
  525.8 18.3 %all-to-all-start.3 = ((bf16[8,1,20,2304]{3,2,1,0:T(8,128)(2,1)}), bf16[8,1,20,2304]{3,2,1,0:T(8,128)(2,1)}, u32[]{:S(2)}, u32[]{:S(2)}) async-start(bf16[8,1,20,2304]{3,2,1,0:T(8,128)(2,1)} %copy.64), calls=%async_computation.4 | async-start | bytes 1769472 | tf_op jit(solution)/shard_map/all_to_all | solution.py:145
  530.0 10.5 %copy-start.5 = (bf16[64,2304]{1,0:T(8,128)(2,1)S(1)}, bf16[64,2304]{1,0:T(8,128)(2,1)}, u32[]{:S(2)}) copy-start(bf16[64,2304]{1,0:T(8,128)(2,1)} %copy-done.4) | copy-start | bytes 884740
  530.0 10.5 %copy-start.9 = (bf16[2304,8]{0,1:T(8,128)(2,1)S(1)}, bf16[2304,8]{0,1:T(8,128)(2,1)}, u32[]{:S(2)}) copy-start(bf16[2304,8]{0,1:T(8,128)(2,1)} %param.21) | copy-start | bytes 110596
  530.1 15.6 %copy-start.3 = (f32[64,2304]{1,0:T(8,128)S(1)}, f32[64,2304]{1,0:T(8,128)}, u32[]{:S(2)}) copy-start(f32[64,2304]{1,0:T(8,128)} %reduce-scatter.5.cloned.1.call-done) | copy-start | bytes 1769476
  545.4 2.1 copy-start.1
Sparse Core Ops, SparseCore 0:
  22.5 55.6 all-gather.3
  80.4 35.3 all-gather.5
  132.4 62.2 reduce-scatter.4
  218.1 123.7 all-gather.7
  410.3 113.3 reduce-scatter.6
where the time goes:
time: 558 us; the launch traced here: 556 us
  waiting for transfers between devices  286 us (51%)
  local copies, waits for them, and re-layouts  103 us (18%)
  blocking collectives  90.4 us (16%)
  matrix products  39.1 us (7%)
  other arithmetic  17.4 us (3%)
  between operations  15.4 us (3%)
    unnamed x6, waiting for transfers between devices  113 us
    all_to_all x1, blocking collectives, body(): lax.all_to_all(joined, ('group', 'inner'), split_axis=0, concat_axis=2, t...  61.6 us
    reduce_scatter x1, waiting for transfers between devices, body(): lax.psum_scatter(jnp.dot(block_outputs, out_weight, preferred_element_typ...  61.1 us
    all_gather x1, waiting for transfers between devices, body(): server_qkv = lax.all_gather(head_parts, 'group', axis=0, tiled=True)  51.4 us
    all_gather x1, waiting for transfers between devices, body(): piece_rows = lax.all_gather(normed, 'inner', axis=0, tiled=True)  31.8 us
    all_gather x1, waiting for transfers between devices, body(): arrived = lax.all_gather(owned, 'group', axis=0, tiled=True)  24.8 us
    unnamed x30, local copies, waits for them, and re-layouts  19.4 us
    another operation x1, local copies, waits for them, and re-layouts, body(): rows_in = arrived[:, 0].reshape(item_count * capacity, D)  17.2 us
  transfers between devices with their start and end apart: 6, of which 6 were waited for; matrix products, arithmetic and copies ran while one was open for 10% of the time, Pallas kernels for 0%

commit v1 on v0

--- a/solution.py
+++ b/solution.py
@@ -59,7 +59,20 @@
     cast_qkv = trainer_qkv.astype(jnp.bfloat16).reshape(row_share, 3, inner_size, head_block)
     head_parts = lax.all_to_all(cast_qkv, "inner", split_axis=2, concat_axis=0, tiled=True)
     head_parts = head_parts.reshape(inner_size * row_share, 3, head_block)
-    server_qkv = lax.all_gather(head_parts, "group", axis=0, tiled=True)
+
+    def fix_wires_all(a0):
+        g_now = jnp.concatenate(
+            lax.all_to_all(
+                jnp.stack([a0 for _ in range(lax.axis_size("group"))]),
+                split_axis=0,
+                axis_name="group",
+                concat_axis=0,
+            ),
+            axis=0,
+        )
+        return g_now
+
+    server_qkv = fix_wires_all(head_parts)
     expert_count = trainer_gate_up.shape[0]
     local_experts = expert_count // inner_size
     hidden_share = trainer_gate_up.shape[3] // group_size

time: 558 us -> 539 us (0.966)
  waiting for transfers between devices: 286 us -> 246 us
  local copies, waits for them, and re-layouts: 103 us -> 114 us
  starting transfers between devices: 4.61 us -> 14.1 us
    all_gather x1 -> x0, waiting for transfers between devices: 51.4 us -> none  [body(): server_qkv = lax.all_gather(head_parts, 'group', axis=0, tiled=True)]
    all_to_all x0 -> x1, waiting for transfers between devices: none -> 51.4 us  [fix_wires_all(): lax.all_to_all(jnp.stack([a0 for _ in range(lax.axis_size('group'))]), sp...]
    all_gather x1, waiting for transfers between devices: 31.8 us -> 0.01 us  [body(): piece_rows = lax.all_gather(normed, 'inner', axis=0, tiled=True)]
    all_to_all x0 -> x1, starting transfers between devices: none -> 9.71 us  [fix_wires_all(): lax.all_to_all(jnp.stack([a0 for _ in range(lax.axis_size('group'))]), sp...]
    all_to_all x0 -> x2, local copies, waits for them, and re-layouts: none -> 8.64 us  [fix_wires_all(): lax.all_to_all(jnp.stack([a0 for _ in range(lax.axis_size('group'))]), sp...]
    dot_general x0 -> x1, local copies, waits for them, and re-layouts: none -> 5.79 us  [body(): jnp.dot(piece_rows, flat_qkv, preferred_element_type=jnp.float32)]
    all_gather x1 -> x0, local copies, waits for them, and re-layouts: 5.74 us -> none  [body(): server_qkv = lax.all_gather(head_parts, 'group', axis=0, tiled=True)]
    unnamed x30 -> x26, local copies, waits for them, and re-layouts: 19.4 us -> 19.7 us
  transfers between devices with their start and end apart: 6 -> 6, of which waited for: 6 -> 4; matrix products, arithmetic and copies ran while one was open for 10% -> 13% of each run, Pallas kernels for 0% -> 0%
where the time goes in v1:
time: 539 us; the launch traced here: 537 us
  waiting for transfers between devices  246 us (46%)
  local copies, waits for them, and re-layouts  114 us (21%)
  blocking collectives  90.6 us (17%)
  matrix products  38.9 us (7%)
  other arithmetic  18.6 us (3%)
  between operations  15.3 us (3%)
  starting transfers between devices  14.1 us (3%)
    unnamed x5, waiting for transfers between devices  113 us
    all_to_all x1, blocking collectives, body(): lax.all_to_all(joined, ('group', 'inner'), split_axis=0, concat_axis=2, t...  61.4 us
    reduce_scatter x1, waiting for transfers between devices, body(): lax.psum_scatter(jnp.dot(block_outputs, out_weight, preferred_element_typ...  56.3 us
    all_to_all x1, waiting for transfers between devices, fix_wires_all(): lax.all_to_all(jnp.stack([a0 for _ in range(lax.axis_size('group'))]), sp...  51.4 us
    all_gather x1, waiting for transfers between devices, body(): arrived = lax.all_gather(owned, 'group', axis=0, tiled=True)  24.8 us
    unnamed x26, local copies, waits for them, and re-layouts  19.7 us
    another operation x1, local copies, waits for them, and re-layouts, body(): rows_in = arrived[:, 0].reshape(item_count * capacity, D)  17.2 us
    all_to_all x1, blocking collectives, body(): lax.all_to_all(send_rows, 'inner', split_axis=0, concat_axis=0, tiled=True)  16.4 us
  transfers between devices with their start and end apart: 6, of which 4 were waited for; matrix products, arithmetic and copies ran while one was open for 13% of the time, Pallas kernels for 0%

profile of v1, /device:TPU:1, one launch (start us, length us, event | category | flops | bytes accessed | tf_op | source)
XLA Modules:
  0.0 536.6 jit_solution(7101737163148010467)
XLA Ops:
  11.8 12.7 %all_to_all.39 = bf16[18,3,8,256]{3,0,1,2:T(8,128)(2,1)S(1)} all-to-all(bf16[18,3,8,256]{3,0,1,2:T(8,128)(2,1)S(1)} %copy.74), channel_id=1, replica_groups=mesh['group'=16,'inner'=8] {'inner'}, dimensions={2} | all-to-all | bytes 442368 | tf_op jit(solution)/shard_map/all_to_all | solution.py:60
  26.7 9.7 %all-to-all-start.1 = ((bf16[16,144,3,256]{3,1,2,0:T(8,128)(2,1)}), bf16[16,144,3,256]{3,1,2,0:T(8,128)(2,1)}, u32[]{:S(2)}, u32[]{:S(2)}) async-start(bf16[16,144,3,256]{3,1,2,0:T(8,128)(2,1)} %stack.3), calls=%async_computation.1 | async-start | bytes 7077888 | tf_op jit(solution)/shard_map/all_to_all | solution.py:65
  38.9 51.4 %all-to-all-done.1 = bf16[16,144,3,256]{3,1,2,0:T(8,128)(2,1)} async-done(((bf16[16,144,3,256]{3,1,2,0:T(8,128)(2,1)}), bf16[16,144,3,256]{3,1,2,0:T(8,128)(2,1)}, u32[]{:S(2)}, u32[]{:S(2)}) %all-to-all-start.1) | async-done | bytes 3538976 | tf_op jit(solution)/shard_map/all_to_all | solution.py:65
  90.3 4.4 copy.78
  97.6 5.8 %copy.79 = bf16[768,2304]{1,0:T(8,128)(2,1)} copy(bf16[768,2304]{0,1:T(8,128)(2,1)} %bitcast.91) | data formatting | bytes 7077888 | tf_op jit(solution)/shard_map/dot_general | solution.py:95
  103.4 4.8 fusion.8
  109.2 4.7 fusion.36
  121.1 56.3 %reduce-scatter.5.cloned.1.call-done = f32[64,2304]{1,0:T(8,128)} async-done(((f32[512,2304]{1,0:T(8,128)}), f32[64,2304]{1,0:T(8,128)}) %reduce-scatter.5.cloned.1.call-update) | async-done | bytes 589840 | tf_op jit(solution)/shard_map/reduce_scatter | solution.py:120
  183.6 16.4 %all_to_all.40 = bf16[8,1,20,2304]{3,2,1,0:T(8,128)(2,1)S(1)} all-to-all(bf16[8,1,20,2304]{3,2,1,0:T(8,128)(2,1)S(1)} %bitcast.95), channel_id=1, replica_groups=mesh['group'=16,'inner'=8] {'inner'}, dimensions={0} | all-to-all | bytes 1474560 | tf_op jit(solution)/shard_map/all_to_all | solution.py:145
  201.1 6.9 %convert_element_type.69 = bf16[8,18,2,5760]{3,2,1,0:T(2,128)(2,1)} convert(f32[8,18,2,5760]{3,2,1,0:T(2,128)} %param.16) | non-fusion elementwise | flops 1658880 | bytes 9953280 | tf_op jit(solution)/shard_map/convert_element_type | solution.py:79
  207.9 11.5 %reshape.214 = bf16[8,1,18,2,16,360]{5,4,3,2,0,1:T(8,128)(2,1)} reshape(bf16[8,18,2,5760]{3,2,1,0:T(2,128)(2,1)} %convert_element_type.69) | data formatting | bytes 6635520 | tf_op jit(solution)/shard_map/reshape | solution.py:79
  219.5 4.7 copy.77
  224.2 61.4 %all_to_all.41 = bf16[128,1,1,18,2,360]{5,4,3,2,1,0:T(2,128)(2,1)} all-to-all(bf16[128,1,1,18,2,360]{5,4,3,2,1,0:T(2,128)(2,1)S(1)} %bitcast.90), channel_id=1, replica_groups=mesh['group'=16,'inner'=8] {'group','inner'}, dimensions={0} | all-to-all | bytes 6635520 | tf_op jit(solution)/shard_map/all_to_all | solution.py:84
  285.6 8.5 %reshape_squeeze_reshape.3 = bf16[2304,720]{1,0:T(8,128)(2,1)} reshape(bf16[128,1,1,18,2,360]{5,4,3,2,1,0:T(2,128)(2,1)} %all_to_all.41) | data formatting | bytes 6635520 | tf_op jit(solution)/shard_map/reshape;squeeze;reshape | solution.py:150
  294.1 5.7 %copy.85 = bf16[720,2304]{1,0:T(8,128)(2,1)} copy(bf16[720,2304]{0,1:T(8,128)(2,1)} %bitcast.92) | data formatting | bytes 6635520 | tf_op jit(solution)/shard_map/dot_general | solution.py:149
  299.8 24.8 %all-gather.5.cloned.1.call-done = bf16[128,1,20,2304]{3,0,2,1:T(8,128)(2,1)} async-done(((bf16[8,1,20,2304]{3,0,2,1:T(8,128)(2,1)}), bf16[128,1,20,2304]{3,0,2,1:T(8,128)(2,1)}) %all-gather.5.cloned.1.call-update) | async-done | bytes 11796496 | tf_op jit(solution)/shard_map/all_gather | solution.py:146
  324.5 14.8 %copy.84 = bf16[128,1,20,2304]{3,2,0,1:T(8,128)(2,1)} copy(bf16[128,1,20,2304]{3,0,2,1:T(8,128)(2,1)} %all-gather.5.cloned.1.call-done) | data formatting | bytes 23592960 | tf_op jit(solution)/shard_map/all_gather | solution.py:146
  339.3 17.2 %reshape.224 = bf16[2560,2304,1]{1,0,2:T(8,128)(2,1)} reshape(bf16[128,1,20,2304]{3,2,0,1:T(8,128)(2,1)} %copy.84) | data formatting | bytes 23592960 | tf_op jit(solution)/shard_map/reshape;squeeze | solution.py:148
  356.5 12.7 %fusion.44 = f32[2560,2,360]{0,2,1:T(8,128)S(1)} fusion(bf16[2560,2304,1]{1,0,2:T(8,128)(2,1)} %reshape.224, bf16[2,360,2304]{2,1,0:T(8,128)(2,1)} %bitcast.96), kind=kOutput, calls=%fused_computation.81 | convolution fusion | flops 8493465600 | bytes 22487040 | tf_op jit(solution)/shard_map/dot_general | solution.py:149
  379.4 8.3 %fusion.37 = bf16[16,8,20,2304]{3,1,0,2:T(8,128)(2,1)S(1)} fusion(bf16[1,360,2304]{2,1,0:T(8,128)(2,1)S(1)} %copy-done, bf16[128,20,360]{2,1,0:T(8,128)(2,1)} %convert_element_type.82), kind=kOutput, calls=%fused_computation.78 | convolution fusion | flops 4252631040 | bytes 15298560 | tf_op jit(solution)/shard_map/dot_general | solution.py:154
  387.7 5.1 copy.97
  393.2 113.0 %reduce-scatter.7.cloned.1.call-done = bf16[8,46080]{1,0:T(8,128)(2,1)} async-done(((bf16[128,46080]{1,0:T(8,128)(2,1)}), bf16[8,46080]{1,0:T(8,128)(2,1)}) %reduce-scatter.7.cloned.1.call-update) | async-done | bytes 737296
  508.4 4.2 all-to-all-start.4
  512.6 10.3 %copy.89 = bf16[1,2304,2,360]{1,3,2,0:T(8,128)(2,1)} copy(bf16[1,2304,2,360]{3,2,1,0:T(2,128)(2,1)} %bitcast.88) | data formatting | bytes 6635520
  (78 shorter events, 45.8 us)
Async XLA Ops:
  7.2 372.2 %copy-start = (bf16[1,360,2304]{2,1,0:T(8,128)(2,1)S(1)}, bf16[1,360,2304]{2,1,0:T(8,128)(2,1)}, u32[]{:S(2)}) copy-start(bf16[1,360,2304]{2,1,0:T(8,128)(2,1)} %param.18) | copy-start | bytes 4976644
  7.2 96.2 %all-gather.3.cloned.1.call-start = ((), (), s32[]{:S(2)}) async-start(), calls=%async_computation.7 | async-start | bytes 2654208 | tf_op jit(solution)/shard_map/all_gather | solution.py:93
  26.7 63.6 %all-to-all-start.1 = ((bf16[16,144,3,256]{3,1,2,0:T(8,128)(2,1)}), bf16[16,144,3,256]{3,1,2,0:T(8,128)(2,1)}, u32[]{:S(2)}, u32[]{:S(2)}) async-start(bf16[16,144,3,256]{3,1,2,0:T(8,128)(2,1)} %stack.3), calls=%async_computation.1 | async-start | bytes 7077888 | tf_op jit(solution)/shard_map/all_to_all | solution.py:65
  36.4 141.0 %reduce-scatter.5.cloned.1.call-start = ((), (), s32[]{:S(2)}) async-start(), calls=%async_computation.8 | async-start | bytes 5308416 | tf_op jit(solution)/shard_map/reduce_scatter | solution.py:120
  103.4 4.9 copy-start.6
  103.4 4.9 copy-start.7
  113.9 2.8 copy-start.5
  119.7 0.7 copy-start.10
  119.7 57.7 %copy-start.1 = (bf16[1,64,2304]{2,1,0:T(8,128)(2,1)S(1)}, bf16[1,64,2304]{2,1,0:T(8,128)(2,1)}, u32[]{:S(2)}) copy-start(bf16[1,64,2304]{2,1,0:T(8,128)(2,1)} %param.11) | copy-start | bytes 884740
  119.7 59.0 %copy-start.9 = (f32[2304]{0:T(1024)S(1)}, f32[2304]{0:T(1024)}, u32[]{:S(2)}) copy-start(f32[2304]{0:T(1024)} %param.20) | copy-start | bytes 27652
  119.7 204.8 %all-gather.5.cloned.1.call-start = ((), (), s32[]{:S(2)}) async-start(), calls=%async_computation.9 | async-start | bytes 12533760 | tf_op jit(solution)/shard_map/all_gather | solution.py:146
  179.9 0.7 copy-start.3
  201.0 305.2 %reduce-scatter.7.cloned.1.call-start = ((), (), s32[]{:S(2)}) async-start(), calls=%async_computation.10 | async-start | bytes 12533760
  508.4 19.1 %all-to-all-start.4 = ((bf16[8,1,20,2304]{3,2,1,0:T(8,128)(2,1)}), bf16[8,1,20,2304]{3,2,1,0:T(8,128)(2,1)}, u32[]{:S(2)}, u32[]{:S(2)}) async-start(bf16[8,1,20,2304]{3,2,1,0:T(8,128)(2,1)} %copy.88), calls=%async_computation.5 | async-start | bytes 1769472 | tf_op jit(solution)/shard_map/all_to_all | solution.py:158
  523.0 4.2 copy-start.4
  523.0 4.2 copy-start.8
  523.0 6.1 %copy-start.2 = (f32[64,2304]{1,0:T(8,128)S(1)}, f32[64,2304]{1,0:T(8,128)}, u32[]{:S(2)}) copy-start(f32[64,2304]{1,0:T(8,128)} %reduce-scatter.5.cloned.1.call-done) | copy-start | bytes 1769476
Sparse Core Ops, SparseCore 0:
  10.4 44.2 all-gather.2
  119.8 57.5 reduce-scatter.4
  201.1 123.3 all-gather.4
  393.0 113.1 reduce-scatter.6
